TPU v7x, 32 devices: a whole 2x2x4 slice. The times are simulated.
32 devices in a mesh: panel: 2 (over y), gx: 16 (over z, x, core).
Axes of the slice: x: 2, y: 2, z: 4, core: 2. Of those that a mesh axis runs over, the one named last changes fastest.
Arguments:
- right_side: float32 [20, 1024, 256], P(None, 'gx', 'panel'), may hold values from -40 to 40
- previous: float32 [20, 1024, 256], P(None, 'gx', 'panel'), may hold values from -1.8 to 1.8
- diagonal: float32 [20, 1024, 256], P(None, 'gx', 'panel'), may hold values from 0.5 to 2
- vertical: float32 [19, 1024, 256], P(None, 'gx', 'panel'), may hold values from 0.5 to 2
- metric_a: float32 [1024, 256], P('gx', 'panel'), may hold values from 0.5 to 2
- metric_b: float32 [1024, 256], P('gx', 'panel'), may hold values from 0.5 to 2
- profile: float32 [20], replicated, may hold values from 0.5 to 2
- column_inverse: bfloat16 [4, 20, 1024, 256], P(None, None, 'gx', 'panel'), may hold values from -0.125 to 0.625, as said below
- edge_turn: int32 [4, 16, 2], replicated, may hold values from 0 to 3
Outputs:
- increment: float32 [20, 1024, 256], P(None, 'gx', 'panel')
Inputs may be any that keep to these rules, and one draw needn't show every extreme that they name: Entry column_inverse[c, k] lies in row k mod 4, column c of the inverse of the block of 4 levels that holds level k. `edge_turn`: entries 0 and 2 are read only for their lowest bit; entries 1 and 3 reverse with the lowest bit and negate with the value 2 bit.
All inputs are finite; a program needn't handle non-finite values.
Results may differ from a plain program's by a relative error of at most 0.0003.
Values sent between devices are 32-bit elements; how exact they have to be, the bound alone decides.
A program may use at most 64 MiB of HBM per device.

v0:
```python
import jax
import jax.numpy as jnp
from jax import lax
from jax.sharding import PartitionSpec as P

BK = 4


def from_behind(block, axis, distance):
    devices = range(lax.axis_size(axis))
    route = [((i - distance) % len(devices), i) for i in devices]
    return lax.ppermute(block, axis, route)


def flip_where(condition, values, dimension):
    return jnp.where(condition, jnp.flip(values, dimension), values)


def orient(values, code):
    turned = flip_where(code % 2 == 1, values, 1)
    return jnp.where(code // 2 == 1, -turned, turned)


def from_gx(values, offset):
    return from_behind(values, "gx", offset)


def from_panel(values, offset):
    return from_behind(values, "panel", offset)


def assemble(pressure, diagonal, vertical, flux_a, flux_b, high_a, high_b):
    next_a = jnp.concatenate([flux_a[:, 1:], high_a[:, None]], axis=1)
    next_b = jnp.concatenate([flux_b[:, :, 1:], high_b[:, :, None]], axis=2)
    vertical_flux = vertical * (pressure[1:] - pressure[:-1])
    zeros_row = jnp.zeros((1,) + pressure.shape[1:], jnp.float32)
    upward = jnp.concatenate([zeros_row, vertical_flux], axis=0) - jnp.concatenate(
        [vertical_flux, zeros_row], axis=0
    )
    return diagonal * pressure + (flux_a - next_a + flux_b - next_b) + upward


def local_fluxes(pressure, low_a, low_b, face_a, face_b):
    prev_a = jnp.concatenate([low_a[:, None], pressure[:, :-1]], axis=1)
    prev_b = jnp.concatenate([low_b[:, :, None], pressure[:, :, :-1]], axis=2)
    return (face_a * (pressure - prev_a), face_b * (pressure - prev_b))


def precondition(resid, column_inverse):
    level_count, rows_here, cols_here = resid.shape
    blocks = resid.reshape(level_count // BK, BK, rows_here, cols_here)
    inverse = column_inverse.reshape(BK, level_count // BK, BK, rows_here, cols_here)
    result = inverse[0].astype(jnp.float32) * blocks[:, 0:1]
    for column in range(1, BK):
        result = result + inverse[column].astype(jnp.float32) * blocks[:, column : column + 1]
    return result.reshape(level_count, rows_here, cols_here)


def shards(
    right_side, previous, diagonal, vertical, metric_a, metric_b, profile, column_inverse, edge_turn
):
    gx_index = lax.axis_index("gx")
    panel_index = lax.axis_index("panel")
    turns = edge_turn[:, gx_index, panel_index]
    face_a = metric_a[None] * profile[:, None, None]
    face_b = metric_b[None] * profile[:, None, None]

    def operate(pressure):
        low_a = flip_where(turns[0] % 2 == 1, from_gx(pressure[:, -1], 1), 1)
        low_b = flip_where(turns[2] % 2 == 1, from_panel(pressure[:, :, -1], 1), 1)
        flux_a, flux_b = local_fluxes(pressure, low_a, low_b, face_a, face_b)
        high_a = orient(from_gx(flux_a[:, 0], -1), turns[1])
        high_b = orient(from_panel(flux_b[:, :, 0], -1), turns[3])
        return assemble(pressure, diagonal, vertical, flux_a, flux_b, high_a, high_b)

    resid_first = right_side - operate(previous)
    search_first = precondition(resid_first, column_inverse)
    image_first = operate(search_first)
    cross_first, square_first = lax.psum(
        (jnp.sum(resid_first * image_first), jnp.sum(image_first * image_first)), ("panel", "gx")
    )
    alpha_first = cross_first / square_first
    resid_second = resid_first - alpha_first * image_first
    search_second = precondition(resid_second, column_inverse)
    image_second = operate(search_second)
    along_first, image_square, resid_image, resid_along = lax.psum(
        (
            jnp.sum(image_second * image_first),
            jnp.sum(image_second * image_second),
            jnp.sum(resid_second * image_second),
            jnp.sum(resid_second * image_first),
        ),
        ("panel", "gx"),
    )
    beta_coef = along_first / square_first
    alpha_second = (resid_image - beta_coef * resid_along) / (
        image_square - 2.0 * beta_coef * along_first + beta_coef * beta_coef * square_first
    )
    direction = search_second - beta_coef * search_first
    return alpha_first * search_first + alpha_second * direction


def solution(mesh):
    return jax.shard_map(
        shards,
        mesh=mesh,
        in_specs=(
            P(None, "gx", "panel"),
            P(None, "gx", "panel"),
            P(None, "gx", "panel"),
            P(None, "gx", "panel"),
            P("gx", "panel"),
            P("gx", "panel"),
            P(),
            P(None, None, "gx", "panel"),
            P(),
        ),
        out_specs=P(None, "gx", "panel"),
        check_vma=False,
    )
```

profile of v0, /device:TPU:0, one launch (start us, length us, event | category | flops | bytes accessed | tf_op | source)
XLA Modules:
  0.0 173.3 jit_solution(4378615325111884345)
XLA Ops:
  0.0 1.4 slice.165
  1.7 3.0 %collective-permute-start.2 = (f32[20,64]{1,0:T(8,128)S(1)}, f32[20,64]{1,0:T(8,128)S(1)}, u32[]{:S(2)}, u32[]{:S(2)}) collective-permute-start(f32[20,64]{1,0:T(8,128)S(1)} %bitcast.126), channel_id=1, source_target_pairs={{16,0},{0,16},{17,1},{1,17},{18,2},{2,18},{19,3},{3,19},{20,4},{4,... | collective-permute-start | bytes 15368 | tf_op jit(solution)/shard_map/ppermute | solution.py:12
  5.2 1.3 copy_multiply_fusion.2
  17.7 1.3 copy.378
  19.0 2.0 %multiply_multiply_fusion.5 = (f32[20,64,128]{2,0,1:T(8,128)S(1)}, f32[20,64,128]{2,0,1:T(8,128)S(1)}) fusion(f32[20,63,128]{2,0,1:T(8,128)} %slice.205, f32[20,1,128]{2,0,1:T(8,128)S(1)} %select_bitcast_fusion.5, f32[20]{0:T(128)S(1)} %copy-done.15, f32[64,128]{1,0:T(8,128)S(1)} %copy-done.13, f32[20,64,128]{2,1,0:T(8,128)S(1)} %copy-done, ...), kind=kLoop, calls=%fused_computation.5 | loop fusion | flops 1310720 | bytes 3342416 | tf_op jit(solution)/shard_map/mul | solution.py:46
  23.7 4.2 %collective-permute-start.1 = (f32[20,128]{1,0:T(8,128)S(1)}, f32[20,128]{1,0:T(8,128)S(1)}, u32[]{:S(2)}, u32[]{:S(2)}) collective-permute-start(f32[20,128]{1,0:T(8,128)S(1)} %slice_bitcast_fusion.12), channel_id=1, source_target_pairs={{1,0},{2,1},{3,2},{4,3},{5,4},{6,5},{7,6},{8,7},{9,8},{10,9},{11,1... | collective-permute-start | bytes 30728 | tf_op jit(solution)/shard_map/ppermute | solution.py:12
  28.0 1.3 copy.381
  29.4 3.8 %fusion.2 = f32[20,64,128]{2,0,1:T(8,128)S(1)} fusion(f32[20,64,128]{2,1,0:T(8,128)} %param.11, f32[20,64,128]{2,0,1:T(8,128)S(1)} %get-tuple-element.27, f32[20,64,128]{2,0,1:T(8,128)S(1)} %get-tuple-element.26, f32[20,1,128]{2,0,1:T(8,128)S(1)} %fusion.19, f32[20,63,128]{2,0,1:T(8,128)} %slice.206, f32[20,64,1]{2,0,1:T(8,128)} %copy.381, ...), kind=kLoop, calls=%fused_computation.22 | loop fusion | flops 1638400 | bytes 5865472 | tf_op jit(solution)/shard_map/sub | solution.py:76
  34.6 2.1 %fusion.9 = f32[20,64,128]{2,0,1:T(8,128)S(1)} fusion(f32[20,64,128]{2,1,0:T(8,128)S(1)} %bitcast.116, f32[20,64,128]{2,1,0:T(8,128)S(1)} %bitcast.118, f32[20,64,128]{2,1,0:T(8,128)S(1)} %bitcast.119, f32[20,64,128]{2,1,0:T(8,128)S(1)} %bitcast.115, bf16[1,20,64,128]{3,2,1,0:T(8,128)(2,1)S(1)} %copy-done.10, bf16[1,20,64,128]{3,2,1,0:T(8,128)(2,1)S(1)} %copy-done.8, ...), kind=kLoop, calls=%fused_computation.29 | loop fusion | flops 1802240 | bytes 4587520 | tf_op jit(solution)/shard_map/add | solution.py:55
  36.8 1.4 copy_multiply_fusion.1
  38.8 1.8 %collective-permute-start.6 = (f32[20,64]{1,0:T(8,128)S(1)}, f32[20,64]{1,0:T(8,128)S(1)}, u32[]{:S(2)}, u32[]{:S(2)}) collective-permute-start(f32[20,64]{1,0:T(8,128)S(1)} %bitcast.124), channel_id=1, source_target_pairs={{16,0},{0,16},{17,1},{1,17},{18,2},{2,18},{19,3},{3,19},{20,4},{4,... | collective-permute-start | bytes 15368 | tf_op jit(solution)/shard_map/ppermute | solution.py:12
  42.6 1.3 copy.397
  43.8 3.5 %collective-permute-done.4 = f32[20,128]{1,0:T(8,128)S(1)} collective-permute-done((f32[20,128]{1,0:T(8,128)S(1)}, f32[20,128]{1,0:T(8,128)S(1)}, u32[]{:S(2)}, u32[]{:S(2)}) %collective-permute-start.4) | collective-permute-done | bytes 10272 | tf_op jit(solution)/shard_map/ppermute | solution.py:12
  47.4 1.7 multiply_multiply_fusion.4
  56.8 3.9 %multiply_reduce_fusion.4 = (f32[]{:T(128)}, f32[]{:T(128)}, f32[20,64,128]{2,0,1:T(8,128)S(1)}) fusion(f32[20,64,128]{2,0,1:T(8,128)S(1)} %fusion.2, f32[19,64,128]{2,0,1:T(8,128)} %copy_multiply_fusion.1, f32[20,64,1]{2,0,1:T(8,128)} %copy.399, f32[20,64,127]{2,0,1:T(8,128)} %slice.223, f32[20,64,128]{2,0,1:T(8,128)S(1)} %get-tuple-element.25, ...), kind=kLoop, calls=%fused_computation.57 | loop fusion | flops 2129918 | bytes 5865480 | tf_op jit(solution)/shard_map/reduce_sum | solution.py:80
  60.7 37.9 %all-reduce.7 = (f32[]{:T(128)}, f32[]{:T(128)}) all-reduce(f32[]{:T(128)} %get-tuple-element.10, f32[]{:T(128)} %get-tuple-element.9), channel_id=1, replica_groups=mesh['panel'=2,'gx'=16] {'panel','gx'}, use_global_device_ids=true, to_apply=%region_1.2 | all-reduce | flops 2 | bytes 16 | tf_op jit(solution)/shard_map/psum | solution.py:79
  102.2 2.1 %fusion.12 = f32[20,64,128]{2,0,1:T(8,128)S(1)} fusion(f32[20,64,128]{2,1,0:T(8,128)S(1)} %bitcast.113, f32[20,64,128]{2,1,0:T(8,128)S(1)} %bitcast.114, f32[20,64,128]{2,1,0:T(8,128)S(1)} %bitcast.117, f32[20,64,128]{2,1,0:T(8,128)S(1)} %bitcast.112, bf16[1,20,64,128]{3,2,1,0:T(8,128)(2,1)S(1)} %copy-done.11, bf16[1,20,64,128]{3,2,1,0:T(8,128)(2,1)S(1)} %copy-done.9, ...), kind=kLoop, calls=%fused_computation.32 | loop fusion | flops 1802240 | bytes 4587520 | tf_op jit(solution)/shard_map/add | solution.py:55
  104.4 1.4 copy_multiply_fusion
  106.3 2.6 %collective-permute-start.10 = (f32[20,64]{1,0:T(8,128)S(1)}, f32[20,64]{1,0:T(8,128)S(1)}, u32[]{:S(2)}, u32[]{:S(2)}) collective-permute-start(f32[20,64]{1,0:T(8,128)S(1)} %bitcast.125), channel_id=1, source_target_pairs={{16,0},{0,16},{17,1},{1,17},{18,2},{2,18},{19,3},{3,19},{20,4},{4,... | collective-permute-start | bytes 15368 | tf_op jit(solution)/shard_map/ppermute | solution.py:12
  111.9 3.8 %collective-permute-done.8 = f32[20,128]{1,0:T(8,128)S(1)} collective-permute-done((f32[20,128]{1,0:T(8,128)S(1)}, f32[20,128]{1,0:T(8,128)S(1)}, u32[]{:S(2)}, u32[]{:S(2)}) %collective-permute-start.8) | collective-permute-done | bytes 10272 | tf_op jit(solution)/shard_map/ppermute | solution.py:12
  115.8 2.6 %multiply_multiply_fusion.3 = (f32[20,64,128]{2,0,1:T(8,128)}, f32[20,64,128]{2,0,1:T(8,128)S(1)}) fusion(f32[20,64,128]{2,0,1:T(8,128)S(1)} %fusion.12, f32[20,63,128]{2,0,1:T(8,128)} %slice.232, f32[20,1,128]{2,0,1:T(8,128)S(1)} %select_bitcast_fusion.1, f32[20]{0:T(128)S(1)} %copy-done.15, f32[64,128]{1,0:T(8,128)S(1)} %copy-done.13, ...), kind=kLoop, calls=%fused_computation.3 | loop fusion | flops 1310720 | bytes 3342416 | tf_op jit(solution)/shard_map/mul | solution.py:46
  119.4 2.1 %slice.233 = f32[20,63,128]{2,0,1:T(8,128)} slice(f32[20,64,128]{2,0,1:T(8,128)} %get-tuple-element.22), slice={[0:20], [1:64], [0:128]} | slice | bytes 1290240 | tf_op jit(solution)/shard_map/slice | solution.py:33
  124.2 4.3 %multiply_reduce_fusion = (f32[]{:T(128)}, f32[]{:T(128)}, f32[]{:T(128)}, f32[]{:T(128)}) fusion(f32[20,64,128]{2,0,1:T(8,128)S(1)} %get-tuple-element.17, f32[20,64,128]{2,0,1:T(8,128)} %copy-done.2, f32[19,64,128]{2,0,1:T(8,128)} %copy_multiply_fusion, f32[20,64,1]{2,0,1:T(8,128)} %copy.410, f32[20,64,127]{2,0,1:T(8,128)} %slice.237, ...), kind=kLoop, calls=%fused_computation.52 | loop fusion | flops 2785276 | bytes 5865488 | tf_op jit(solution)/shard_map/reduce_sum | solution.py:89
  128.4 39.3 %all-reduce.6 = (f32[]{:T(128)}, f32[]{:T(128)}, f32[]{:T(128)}, f32[]{:T(128)}) all-reduce(f32[]{:T(128)} %get-tuple-element.6, f32[]{:T(128)} %get-tuple-element.8, f32[]{:T(128)} %get-tuple-element.7, f32[]{:T(128)} %get-tuple-element.5), channel_id=1, replica_groups=mesh['panel'=2,'gx'=16] {'panel','gx'}, use_global_device_ids=true, to_apply=%region_7.8 | all-reduce | flops 4 | bytes 32 | tf_op jit(solution)/shard_map/psum | solution.py:86
  (119 shorter events, 28.8 us)
Async XLA Ops:
  0.0 4.7 %copy-start = (f32[20,64,128]{2,1,0:T(8,128)S(1)}, f32[20,64,128]{2,1,0:T(8,128)}, u32[]{:S(2)}) copy-start(f32[20,64,128]{2,1,0:T(8,128)} %param.10) | copy-start | bytes 1966084
  1.4 3.8 %copy-start.3 = (f32[19,64,128]{2,1,0:T(8,128)S(1)}, f32[19,64,128]{2,1,0:T(8,128)}, u32[]{:S(2)}) copy-start(f32[19,64,128]{2,1,0:T(8,128)} %param.12) | copy-start | bytes 1867780
  1.7 15.9 %collective-permute-start.2 = (f32[20,64]{1,0:T(8,128)S(1)}, f32[20,64]{1,0:T(8,128)S(1)}, u32[]{:S(2)}, u32[]{:S(2)}) collective-permute-start(f32[20,64]{1,0:T(8,128)S(1)} %bitcast.126), channel_id=1, source_target_pairs={{16,0},{0,16},{17,1},{1,17},{18,2},{2,18},{19,3},{3,19},{20,4},{4,... | collective-permute-start | bytes 15368 | tf_op jit(solution)/shard_map/ppermute | solution.py:12
  5.1 13.8 %collective-permute-start = (f32[20,128]{1,0:T(8,128)S(1)}, f32[20,128]{1,0:T(8,128)S(1)}, u32[]{:S(2)}, u32[]{:S(2)}) collective-permute-start(f32[20,128]{1,0:T(8,128)S(1)} %slice_bitcast_fusion.13), channel_id=1, source_target_pairs={{15,0},{0,1},{1,2},{2,3},{3,4},{4,5},{5,6},{6,7},{7,8},{8,9},{9,10... | collective-permute-start | bytes 30728 | tf_op jit(solution)/shard_map/ppermute | solution.py:12
  5.2 1.3 copy-start.12
  8.2 10.8 %copy-start.13 = (f32[64,128]{1,0:T(8,128)S(1)}, f32[64,128]{1,0:T(8,128)}, u32[]{:S(2)}) copy-start(f32[64,128]{1,0:T(8,128)} %param.13) | copy-start | bytes 98308
  8.2 10.8 %copy-start.14 = (f32[64,128]{1,0:T(8,128)S(1)}, f32[64,128]{1,0:T(8,128)}, u32[]{:S(2)}) copy-start(f32[64,128]{1,0:T(8,128)} %param.14) | copy-start | bytes 98308
  8.2 10.8 %copy-start.15 = (f32[20]{0:T(128)S(1)}, f32[20]{0:T(128)}, u32[]{:S(2)}) copy-start(f32[20]{0:T(128)} %param.15) | copy-start | bytes 244
  21.3 6.6 %collective-permute-start.3 = (f32[20,64]{1,0:T(8,128)S(1)}, f32[20,64]{1,0:T(8,128)S(1)}, u32[]{:S(2)}, u32[]{:S(2)}) collective-permute-start(f32[20,64]{1,0:T(8,128)S(1)} %bitcast.122), channel_id=1, source_target_pairs={{16,0},{0,16},{17,1},{1,17},{18,2},{2,18},{19,3},{3,19},{20,4},{4,... | collective-permute-start | bytes 15368 | tf_op jit(solution)/shard_map/ppermute | solution.py:12
  23.7 5.6 %collective-permute-start.1 = (f32[20,128]{1,0:T(8,128)S(1)}, f32[20,128]{1,0:T(8,128)S(1)}, u32[]{:S(2)}, u32[]{:S(2)}) collective-permute-start(f32[20,128]{1,0:T(8,128)S(1)} %slice_bitcast_fusion.12), channel_id=1, source_target_pairs={{1,0},{2,1},{3,2},{4,3},{5,4},{6,5},{7,6},{8,7},{9,8},{10,9},{11,1... | collective-permute-start | bytes 30728 | tf_op jit(solution)/shard_map/ppermute | solution.py:12
  33.5 1.1 copy-start.8
  33.5 1.2 copy-start.10
  34.6 2.1 %copy-start.4 = (f32[19,64,128]{2,1,0:T(8,128)S(1)}, f32[19,64,128]{2,1,0:T(8,128)}, u32[]{:S(2)}) copy-start(f32[19,64,128]{2,1,0:T(8,128)} %param.12) | copy-start | bytes 1867780
  38.8 3.7 %collective-permute-start.6 = (f32[20,64]{1,0:T(8,128)S(1)}, f32[20,64]{1,0:T(8,128)S(1)}, u32[]{:S(2)}, u32[]{:S(2)}) collective-permute-start(f32[20,64]{1,0:T(8,128)S(1)} %bitcast.124), channel_id=1, source_target_pairs={{16,0},{0,16},{17,1},{1,17},{18,2},{2,18},{19,3},{3,19},{20,4},{4,... | collective-permute-start | bytes 15368 | tf_op jit(solution)/shard_map/ppermute | solution.py:12
  41.5 5.8 %collective-permute-start.4 = (f32[20,128]{1,0:T(8,128)S(1)}, f32[20,128]{1,0:T(8,128)S(1)}, u32[]{:S(2)}, u32[]{:S(2)}) collective-permute-start(f32[20,128]{1,0:T(8,128)S(1)} %slice_bitcast_fusion.11), channel_id=1, source_target_pairs={{15,0},{0,1},{1,2},{2,3},{3,4},{4,5},{5,6},{6,7},{7,8},{8,9},{9,10... | collective-permute-start | bytes 30728 | tf_op jit(solution)/shard_map/ppermute | solution.py:12
  49.1 3.9 %copy-start.1 = (f32[20,64,128]{2,0,1:T(8,128)}, f32[20,64,128]{2,0,1:T(8,128)S(1)}, u32[]{:S(2)}) copy-start(f32[20,64,128]{2,0,1:T(8,128)S(1)} %get-tuple-element.24) | copy-start | bytes 1966084
  50.0 4.0 %collective-permute-start.7 = (f32[20,64]{1,0:T(8,128)}, f32[20,64]{1,0:T(8,128)}, u32[]{:S(2)}, u32[]{:S(2)}) collective-permute-start(f32[20,64]{1,0:T(8,128)} %bitcast.31), channel_id=1, source_target_pairs={{16,0},{0,16},{17,1},{1,17},{18,2},{2,18},{19,3},{3,19},{20,4},{4,... | collective-permute-start | bytes 15368 | tf_op jit(solution)/shard_map/ppermute | solution.py:12
  53.0 3.7 %collective-permute-start.5 = (f32[20,128]{1,0:T(8,128)}, f32[20,128]{1,0:T(8,128)S(1)}, u32[]{:S(2)}, u32[]{:S(2)}) collective-permute-start(f32[20,128]{1,0:T(8,128)} %slice_bitcast_fusion.10), channel_id=1, source_target_pairs={{1,0},{2,1},{3,2},{4,3},{5,4},{6,5},{7,6},{8,7},{9,8},{10,9},{11,1... | collective-permute-start | bytes 30728 | tf_op jit(solution)/shard_map/ppermute | solution.py:12
  101.1 1.2 copy-start.11
  102.2 2.1 %copy-start.5 = (f32[19,64,128]{2,1,0:T(8,128)S(1)}, f32[19,64,128]{2,1,0:T(8,128)}, u32[]{:S(2)}) copy-start(f32[19,64,128]{2,1,0:T(8,128)} %param.12) | copy-start | bytes 1867780
  106.3 4.2 %collective-permute-start.10 = (f32[20,64]{1,0:T(8,128)S(1)}, f32[20,64]{1,0:T(8,128)S(1)}, u32[]{:S(2)}, u32[]{:S(2)}) collective-permute-start(f32[20,64]{1,0:T(8,128)S(1)} %bitcast.125), channel_id=1, source_target_pairs={{16,0},{0,16},{17,1},{1,17},{18,2},{2,18},{19,3},{3,19},{20,4},{4,... | collective-permute-start | bytes 15368 | tf_op jit(solution)/shard_map/ppermute | solution.py:12
  109.9 5.8 %collective-permute-start.8 = (f32[20,128]{1,0:T(8,128)S(1)}, f32[20,128]{1,0:T(8,128)S(1)}, u32[]{:S(2)}, u32[]{:S(2)}) collective-permute-start(f32[20,128]{1,0:T(8,128)S(1)} %slice_bitcast_fusion.9), channel_id=1, source_target_pairs={{15,0},{0,1},{1,2},{2,3},{3,4},{4,5},{5,6},{6,7},{7,8},{8,9},{9,10... | collective-permute-start | bytes 30728 | tf_op jit(solution)/shard_map/ppermute | solution.py:12
  118.7 4.0 %collective-permute-start.11 = (f32[20,64]{1,0:T(8,128)S(1)}, f32[20,64]{1,0:T(8,128)S(1)}, u32[]{:S(2)}, u32[]{:S(2)}) collective-permute-start(f32[20,64]{1,0:T(8,128)S(1)} %bitcast.123), channel_id=1, source_target_pairs={{16,0},{0,16},{17,1},{1,17},{18,2},{2,18},{19,3},{3,19},{20,4},{4,... | collective-permute-start | bytes 15368 | tf_op jit(solution)/shard_map/ppermute | solution.py:12
  122.7 1.4 collective-permute-start.9
  (5 other events, 4.9 us)
where the time goes:
time: 175 us; the launch traced here: 173 us
  blocking collectives  77.2 us (44%)
  local copies, waits for them, and re-layouts  31.4 us (18%)
  other arithmetic  27.7 us (16%)
  between operations  14.6 us (8%)
  starting transfers between devices  13.2 us (8%)
  waiting for transfers between devices  9.2 us (5%)
    psum x1, blocking collectives, shards(): lax.psum((jnp.sum(image_second * image_first), jnp.sum(image_second * ima...  39.3 us
    psum x1, blocking collectives, shards(): lax.psum((jnp.sum(resid_first * image_first), jnp.sum(image_first * image...  37.9 us
    ppermute x12, starting transfers between devices, from_behind(): return lax.ppermute(block, axis, route)  13.2 us
    ppermute x12, waiting for transfers between devices, from_behind(): return lax.ppermute(block, axis, route)  9.2 us
    mul x3, other arithmetic, local_fluxes(): return (face_a * (pressure - prev_a), face_b * (pressure - prev_b))  6.3 us
    reduce_sum x1, other arithmetic, shards(): jnp.sum(image_second * image_second)  4.28 us
    add x2, other arithmetic, precondition(): result + inverse[column].astype(jnp.float32) * blocks[:, column:column + 1]  4.25 us
    mul x3, other arithmetic, assemble(): vertical_flux = vertical * (pressure[1:] - pressure[:-1])  4.12 us
  transfers between devices with their start and end apart: 12, of which 6 were waited for; matrix products, arithmetic and copies ran while one was open for 14% of the time, Pallas kernels for 0%

commit v1 on v0

v1 whole, which is shorter than its diff:
```python
import functools

import jax
import jax.numpy as jnp
from jax import lax
from jax.experimental import pallas as pl
from jax.experimental.pallas import tpu as pltpu
from jax.sharding import PartitionSpec as P

BK = 4
PAD = 8
CH = 16
MESH = pl.DeviceIdType.MESH
F32 = jnp.float32


def rev_lanes(x):
    lanes = x.shape[1]
    index = lanes - 1 - lax.broadcasted_iota(jnp.int32, x.shape, 1)
    return jnp.take_along_axis(x, index, axis=1, mode="promise_in_bounds")


def rev_rows(x):
    rows = x.shape[0]
    parts = []
    for start in range(rows - 8, -1, -8):
        part = x[start : start + 8]
        index = 7 - lax.broadcasted_iota(jnp.int32, part.shape, 0)
        parts.append(jnp.take_along_axis(part, index, axis=0, mode="promise_in_bounds"))
    return jnp.concatenate(parts, axis=0)


def odd(code, shape):
    return jnp.full(shape, code & 1, jnp.int32) == 1


def sign_of(code, shape):
    return jnp.where(jnp.full(shape, code & 2, jnp.int32) == 2, -1.0, 1.0).astype(F32)


def kernel(
    n_panel, n_gx,
    right_h, prev_h, diag_h, vert_h, ma_h, mb_h, prof_s, inv_h, turn_s,
    out_ref,
    rs, pp, ss, ww, rr, qq, dg, vt, ma, mb, inv,
    sf, sl, sb, rl, rh, bl, bh, wpk, nma_v, nmb_v,
    row_out, row_in,
    in_sem, rf_send, rl_send, rl_recv, rh_recv, bu_send, bd_send, bl_recv, bh_recv,
    ar_send, ar_recv,
):
    levels, ta, tb = rs.shape
    n_dev = n_panel * n_gx
    g = lax.axis_index("gx")
    q = lax.axis_index("panel")
    me = q * n_gx + g
    g_next, g_prev = lax.rem(g + 1, n_gx), lax.rem(g + n_gx - 1, n_gx)
    q_next, q_prev = lax.rem(q + 1, n_panel), lax.rem(q + n_panel - 1, n_panel)
    one_pair = n_panel == 2

    loads = [
        pltpu.make_async_copy(prev_h, pp.at[:, pl.ds(PAD, ta), :], in_sem.at[0]),
        pltpu.make_async_copy(ma_h, ma.at[pl.ds(0, ta), :], in_sem.at[1]),
        pltpu.make_async_copy(mb_h, mb, in_sem.at[2]),
        pltpu.make_async_copy(diag_h, dg, in_sem.at[3]),
        pltpu.make_async_copy(vert_h, vt, in_sem.at[4]),
        pltpu.make_async_copy(right_h, rs, in_sem.at[5]),
        pltpu.make_async_copy(inv_h, inv, in_sem.at[6]),
    ]
    for load in loads:
        load.start()

    barrier = pltpu.get_barrier_semaphore()

    def greet(i, carry):
        other = lax.rem(me + i, n_dev)
        pl.semaphore_signal(
            barrier, inc=1, device_id=(other // n_gx, lax.rem(other, n_gx)), device_id_type=MESH
        )
        return carry

    lax.fori_loop(1, n_dev, greet, 0)

    t0, t1, t2, t3 = (turn_s[e, g, q] for e in range(4))
    t0n = turn_s[0, g_next, q]
    t2n = turn_s[2, g, q_next]
    rows_shape = sf.shape[1:]
    cols_shape = (ta, tb)

    ma[pl.ds(ta, 8), :] = jnp.ones((8, tb), F32)
    zeros_rows = jnp.zeros(rows_shape, F32)
    for j in range(3):
        sf[j] = zeros_rows
        sl[j] = zeros_rows

    lane = lax.broadcasted_iota(jnp.int32, (CH, tb), 1)
    pair = (lane - 1) >> 1
    lane_c = lax.broadcasted_iota(jnp.int32, cols_shape, 1)

    def remote(src, dst, send, recv, device):
        return pltpu.make_async_remote_copy(
            src_ref=src, dst_ref=dst, send_sem=send, recv_sem=recv,
            device_id=device, device_id_type=MESH,
        )

    def row_copies(j):
        return (
            remote(sl.at[j], rl.at[j], rl_send.at[j], rl_recv.at[j], (q, g_next)),
            remote(sf.at[j], rh.at[j], rf_send.at[j], rh_recv.at[j], (q, g_prev)),
        )

    def col_copies(j):
        down = remote(sb.at[j], bl.at[j], bu_send.at[j], bl_recv.at[j], (q_next, g))
        if one_pair:
            return (down,)
        return (down, remote(sb.at[j], bh.at[j], bd_send.at[j], bh_recv.at[j], (q_prev, g)))

    copies = []

    def send_rows(j, field):
        for k in range(levels):
            sf[j, pl.ds(k, 1), :] = field[k, pl.ds(PAD, 1), :]
            sl[j, pl.ds(k, 1), :] = field[k, pl.ds(PAD + ta - 1, 1), :]
        for copy in row_copies(j):
            copy.start()
            copies.append(copy)

    def send_cols(j):
        for copy in col_copies(j):
            copy.start()
            copies.append(copy)

    def pack(acc, value, k):
        return jnp.where(pair == k, pltpu.roll(value, 2 * k + 2, 1), acc)

    def receive(j, field):
        mine = sl[j]
        mine = jnp.where(odd(t0n, rows_shape), rev_lanes(mine), mine)
        mine_c = pltpu.roll(sb[j], 1, 1)
        mine_c = jnp.where(odd(t2n, cols_shape), rev_rows(mine_c), mine_c)
        for copy in col_copies(j):
            copy.wait_recv()
        from_low = bl[j]
        from_high = bl[j] if one_pair else bh[j]
        if j == 0:
            nmb_v[...] = jnp.broadcast_to(from_high[:, tb - 1 : tb], cols_shape)
        low_c = jnp.where(odd(t2, cols_shape), rev_rows(from_low), from_low)
        high_c = nmb_v[...] * (from_high - mine_c)
        high_c = jnp.where(odd(t3, cols_shape), rev_rows(high_c), high_c) * sign_of(t3, cols_shape)
        wpk[...] = jnp.where(lane_c & 1 == 1, low_c, pltpu.roll(high_c, tb - 2, 1))
        for copy in row_copies(j):
            copy.wait_recv()
        if j == 0:
            nma_v[...] = jnp.broadcast_to(rh[0, pl.ds(levels, 1), :], rows_shape)
        low = rl[j]
        low = jnp.where(odd(t0, rows_shape), rev_lanes(low), low)
        high = nma_v[...] * (rh[j] - mine)
        high = jnp.where(odd(t1, rows_shape), rev_lanes(high), high) * sign_of(t1, rows_shape)
        high = high + sl[j]
        for k in range(levels):
            field[k, pl.ds(PAD - 1, 1), :] = low[k : k + 1]
            field[k, pl.ds(PAD + ta, 1), :] = high[k : k + 1]

    def operate(field, c, emit):
        base = pl.multiple_of(c * CH, CH)
        at = pl.ds(base, CH)
        halo = wpk[at, :]
        ma_here = ma[at, :]
        ma_next = ma[pl.ds(base + 1, CH), :]
        mb_here = mb[at, :]
        below = None
        here = field[0, pl.ds(base + PAD, CH), :]
        for k in range(levels):
            before = field[k, pl.ds(base + PAD - 1, CH), :]
            after = field[k, pl.ds(base + PAD + 1, CH), :]
            edge = pltpu.roll(halo, (tb - 2 * k - 1) % tb, 1)
            left = jnp.where(lane == 0, edge, pltpu.roll(here, 1, 1))
            flux_b = mb_here * (here - left)
            next_b = jnp.where(lane == tb - 1, edge, pltpu.roll(flux_b, tb - 1, 1))
            flux = ma_here * (here - before) - ma_next * (after - here) + (flux_b - next_b)
            value = dg[k, at, :] * here + prof_s[k] * flux
            if below is not None:
                value = value + below
            if k + 1 < levels:
                above = field[k + 1, pl.ds(base + PAD, CH), :]
                vertical = vt[k, at, :] * (above - here)
                value = value - vertical
                below = vertical
            emit(k, here, value, at)
            if k + 1 < levels:
                here = above

    def precondition(block, start, at, store):
        results = []
        for k in range(BK):
            total = None
            for column in range(BK):
                term = inv[column, start + k, at, :].astype(F32) * block[column]
                total = term if total is None else total + term
            results.append(total)
        return results

    zero = jnp.zeros((CH, tb), F32)

    loads[0].wait()
    loads[1].wait()
    loads[2].wait()
    for k in range(1):
        sf[0, pl.ds(levels, 1), :] = ma[pl.ds(0, 1), :]

    def pack_previous(c, carry):
        base = pl.multiple_of(c * CH, CH)
        acc = pltpu.roll(mb[pl.ds(base, CH), :], tb - 1, 1)
        for k in range(levels):
            acc = pack(acc, pp[k, pl.ds(base + PAD, CH), :], k)
        sb[0, pl.ds(base, CH), :] = acc
        return carry

    pl.semaphore_wait(barrier, n_dev - 1)
    send_rows(0, pp)
    lax.fori_loop(0, ta // CH, pack_previous, 0)
    send_cols(0)
    for load in loads[3:]:
        load.wait()
    receive(0, pp)

    def first(c, carry):
        base = pl.multiple_of(c * CH, CH)
        state = {"block": [], "acc": zero}

        def emit(k, here, value, at):
            resid = rs[k, at, :] - value
            rr[k, at, :] = resid
            state["block"].append(resid)
            if len(state["block"]) == BK:
                start = k + 1 - BK
                for i, found in enumerate(precondition(state["block"], start, at, None)):
                    ss[start + i, pl.ds(base + PAD, CH), :] = found
                    state["acc"] = pack(state["acc"], found, start + i)
                state["block"] = []

        operate(pp, c, emit)
        sb[1, pl.ds(base, CH), :] = state["acc"]
        return carry

    lax.fori_loop(0, ta // CH, first, 0)
    send_cols(1)
    send_rows(1, ss)
    receive(1, ss)

    def second(c, carry):
        base = pl.multiple_of(c * CH, CH)
        state = {"block": [], "acc": zero, "rq": carry[0], "qq": carry[1]}

        def emit(k, here, value, at):
            qq[k, at, :] = value
            state["rq"] = state["rq"] + rr[k, at, :] * value
            state["qq"] = state["qq"] + value * value
            state["block"].append(value)
            if len(state["block"]) == BK:
                start = k + 1 - BK
                for i, found in enumerate(precondition(state["block"], start, at, None)):
                    ww[start + i, pl.ds(base + PAD, CH), :] = found
                    state["acc"] = pack(state["acc"], found, start + i)
                state["block"] = []

        operate(ss, c, emit)
        sb[2, pl.ds(base, CH), :] = state["acc"]
        return state["rq"], state["qq"]

    sum_rq, sum_qq = lax.fori_loop(0, ta // CH, second, (zero, zero))
    send_cols(2)
    send_rows(2, ww)
    receive(2, ww)

    def third(c, carry):
        state = {"rv": carry[0], "qv": carry[1], "vv": carry[2]}

        def emit(k, here, value, at):
            state["rv"] = state["rv"] + rr[k, at, :] * value
            state["qv"] = state["qv"] + qq[k, at, :] * value
            state["vv"] = state["vv"] + value * value

        operate(ww, c, emit)
        return state["rv"], state["qv"], state["vv"]

    sum_rv, sum_qv, sum_vv = lax.fori_loop(0, ta // CH, third, (zero, zero, zero))

    lane_1 = lax.broadcasted_iota(jnp.int32, (1, tb), 1)
    mine = jnp.zeros((1, tb), F32)
    for i, part in enumerate((sum_rq, sum_qq, sum_rv, sum_qv, sum_vv)):
        total = jnp.sum(jnp.sum(part, axis=0, keepdims=True), axis=1, keepdims=True)
        mine = jnp.where(lane_1 == i, total, mine)
    row_out[...] = mine

    def share(i, carry):
        other = lax.rem(me + i, n_dev)
        remote(
            row_out, row_in.at[i - 1], ar_send, ar_recv, (other // n_gx, lax.rem(other, n_gx))
        ).start()
        return carry

    lax.fori_loop(1, n_dev, share, 0)
    pltpu.make_async_copy(row_in, row_in, ar_recv).wait()
    sums = mine + jnp.sum(row_in[...], axis=0)

    rq, sq, rv, qv, vv = (sums[:, i : i + 1] for i in range(5))
    ratio = qv / sq
    weight = (rv - ratio * rq) / (vv - ratio * qv)
    on_search = jnp.broadcast_to(rq / sq - weight * ratio, (CH, tb))
    on_second = jnp.broadcast_to(weight, (CH, tb))

    def last(c, carry):
        base = pl.multiple_of(c * CH, CH)
        for k in range(levels):
            out_ref[k, pl.ds(base, CH), :] = (
                on_search * ss[k, pl.ds(base + PAD, CH), :]
                + on_second * ww[k, pl.ds(base + PAD, CH), :]
            )
        return carry

    lax.fori_loop(0, ta // CH, last, 0)
    for copy in copies:
        copy.wait_send()
    pltpu.make_async_copy(row_in, row_in, ar_send).wait()


def solution(mesh):
    n_panel, n_gx = mesh.shape["panel"], mesh.shape["gx"]
    n_dev = n_panel * n_gx

    def shards(right_side, previous, diagonal, vertical, metric_a, metric_b, profile, inverse, turn):
        levels, ta, tb = right_side.shape
        rows = (levels + 1 + 7) // 8 * 8
        vmem = pltpu.VMEM
        dma = pltpu.SemaphoreType.DMA
        field = vmem((levels, ta, tb), F32)
        padded = vmem((levels, ta + 2 * PAD, tb), F32)
        any_spec = pl.BlockSpec(memory_space=pl.ANY)
        smem_spec = pl.BlockSpec(memory_space=pltpu.SMEM)
        return pl.pallas_call(
            functools.partial(kernel, n_panel, n_gx),
            out_shape=jax.ShapeDtypeStruct((levels, ta, tb), F32),
            in_specs=[any_spec] * 6 + [smem_spec, any_spec, smem_spec],
            out_specs=pl.BlockSpec(memory_space=pltpu.VMEM),
            scratch_shapes=[
                field, padded, padded, padded, field, field, field,
                vmem((levels - 1, ta, tb), F32),
                vmem((ta + 8, tb), F32),
                vmem((ta, tb), F32),
                vmem((BK, levels, ta, tb), jnp.bfloat16),
                vmem((3, rows, tb), F32),
                vmem((3, rows, tb), F32),
                vmem((3, ta, tb), F32),
                vmem((3, rows, tb), F32),
                vmem((3, rows, tb), F32),
                vmem((3, ta, tb), F32),
                vmem((3, ta, tb), F32),
                vmem((ta, tb), F32),
                vmem((rows, tb), F32),
                vmem((ta, tb), F32),
                vmem((1, tb), F32),
                vmem((n_dev - 1, 1, tb), F32),
                dma((7,)), dma((3,)), dma((3,)), dma((3,)), dma((3,)),
                dma((3,)), dma((3,)), dma((3,)), dma((3,)),
                dma, dma,
            ],
            compiler_params=pltpu.CompilerParams(
                collective_id=0, has_side_effects=True, vmem_limit_bytes=32 * 1024 * 1024
            ),
        )(right_side, previous, diagonal, vertical, metric_a, metric_b, profile, inverse, turn)

    return jax.shard_map(
        shards,
        mesh=mesh,
        in_specs=(
            P(None, "gx", "panel"),
            P(None, "gx", "panel"),
            P(None, "gx", "panel"),
            P(None, "gx", "panel"),
            P("gx", "panel"),
            P("gx", "panel"),
            P(),
            P(None, None, "gx", "panel"),
            P(),
        ),
        out_specs=P(None, "gx", "panel"),
        check_vma=False,
    )
```

time: 175 us -> 38.7 us (0.22)
  blocking collectives: 77.2 us -> 0 us
  Pallas kernels: 0 us -> 28.8 us
  other arithmetic: 27.7 us -> 0 us
  local copies, waits for them, and re-layouts: 31.4 us -> 9.44 us
  between operations: 14.6 us -> 0.02 us
  starting transfers between devices: 13.2 us -> 0 us
  waiting for transfers between devices: 9.2 us -> 0 us
    psum x2 -> x0, blocking collectives: 77.2 us -> none  [the longest x1 39.3 us: shards(): lax.psum((jnp.sum(image_second * image_first), jnp.sum(image_second * ima...]
    pallas_call x0 -> x1, Pallas kernels: none -> 28.8 us  [shards(): pl.pallas_call(functools.partial(kernel, n_panel, n_gx), out_shape=jax.Sh...]
    slice x19 -> x0, local copies, waits for them, and re-layouts: 16 us -> none  [the longest x3 3.94 us: assemble(): next_a = jnp.concatenate([flux_a[:, 1:], high_a[:, None]], axis=1)]
    ppermute x12 -> x0, starting transfers between devices: 13.2 us -> none  [from_behind(): return lax.ppermute(block, axis, route)]
    mul x6 -> x0, other arithmetic: 10.4 us -> none  [the longest x3 6.3 us: local_fluxes(): return (face_a * (pressure - prev_a), face_b * (pressure - prev_b))]
    ppermute x12 -> x0, waiting for transfers between devices: 9.2 us -> none  [from_behind(): return lax.ppermute(block, axis, route)]
    reduce_sum x2 -> x0, other arithmetic: 8.21 us -> none  [the longest x1 4.28 us: shards(): jnp.sum(image_second * image_second)]
    broadcast_in_dim x6 -> x0, local copies, waits for them, and re-layouts: 7.43 us -> none  [the longest x3 3.73 us: local_fluxes(): prev_b = jnp.concatenate([low_b[:, :, None], pressure[:, :, :-1]], axis=2)]
  transfers between devices with their start and end apart: 12 -> 0, of which waited for: 6 -> 0; matrix products, arithmetic and copies ran while one was open for 14% -> 0% of each run, Pallas kernels for 0% -> 0%
where the time goes in v1:
time: 38.7 us; the launch traced here: 38.2 us
  Pallas kernels  28.8 us (74%)
  local copies, waits for them, and re-layouts  9.44 us (24%)
    pallas_call x1, Pallas kernels, shards(): pl.pallas_call(functools.partial(kernel, n_panel, n_gx), out_shape=jax.Sh...  28.8 us
    unnamed x18, local copies, waits for them, and re-layouts  9.44 us

profile of v1, /device:TPU:0, one launch (start us, length us, event | category | flops | bytes accessed | tf_op | source)
XLA Modules:
  0.0 38.2 jit_solution(5846866838586596257)
XLA Ops:
  0.0 0.8 %copy.10.turn_s = s32[4,16,2]{2,1,0:T(8,128)S(1)} copy(s32[4,16,2]{1,2,0:T(2,128)} %param.17) | data formatting | bytes 1024 | tf_op args[8]
  0.8 0.0 copy-start
  0.8 1.3 %copy-done = bf16[4,20,64,128]{3,2,1,0:T(8,128)(2,1)S(1)} copy-done((bf16[4,20,64,128]{3,2,1,0:T(8,128)(2,1)S(1)}, bf16[4,20,64,128]{3,2,1,0:T(8,128)(2,1)}, u32[]{:S(2)}) %copy-start) | copy-done | bytes 1310744
  2.1 0.0 copy-start.1
  2.1 1.1 %copy-done.1 = f32[20,64,128]{2,1,0:T(8,128)S(1)} copy-done((f32[20,64,128]{2,1,0:T(8,128)S(1)}, f32[20,64,128]{2,1,0:T(8,128)}, u32[]{:S(2)}) %copy-start.1) | copy-done | bytes 655384
  3.2 0.0 copy-start.2
  3.2 1.1 %copy-done.2 = f32[20,64,128]{2,1,0:T(8,128)S(1)} copy-done((f32[20,64,128]{2,1,0:T(8,128)S(1)}, f32[20,64,128]{2,1,0:T(8,128)}, u32[]{:S(2)}) %copy-start.2) | copy-done | bytes 655384
  4.3 0.0 copy-start.3
  4.3 1.1 %copy-done.3 = f32[20,64,128]{2,1,0:T(8,128)S(1)} copy-done((f32[20,64,128]{2,1,0:T(8,128)S(1)}, f32[20,64,128]{2,1,0:T(8,128)}, u32[]{:S(2)}) %copy-start.3) | copy-done | bytes 655384
  5.4 0.0 copy-start.4
  5.4 1.1 %copy-done.4 = f32[19,64,128]{2,1,0:T(8,128)S(1)} copy-done((f32[19,64,128]{2,1,0:T(8,128)S(1)}, f32[19,64,128]{2,1,0:T(8,128)}, u32[]{:S(2)}) %copy-start.4) | copy-done | bytes 622616
  6.4 0.0 copy-start.5
  6.4 0.8 %copy-done.5 = f32[64,128]{1,0:T(8,128)S(1)} copy-done((f32[64,128]{1,0:T(8,128)S(1)}, f32[64,128]{1,0:T(8,128)}, u32[]{:S(2)}) %copy-start.5) | copy-done | bytes 32792
  7.2 0.0 copy-start.6
  7.2 0.8 %copy-done.6 = f32[64,128]{1,0:T(8,128)S(1)} copy-done((f32[64,128]{1,0:T(8,128)S(1)}, f32[64,128]{1,0:T(8,128)}, u32[]{:S(2)}) %copy-start.6) | copy-done | bytes 32792
  8.0 0.0 copy-start.7
  8.0 0.7 %copy-done.7 = f32[20]{0:T(128)S(1)} copy-done((f32[20]{0:T(128)S(1)}, f32[20]{0:T(128)}, u32[]{:S(2)}) %copy-start.7) | copy-done | bytes 104
  8.6 28.8 %shard_map.91 = f32[20,64,128]{2,1,0:T(8,128)S(1)} custom-call(f32[20,64,128]{2,1,0:T(8,128)S(1)} %copy-done.1, f32[20,64,128]{2,1,0:T(8,128)S(1)} %copy-done.2, f32[20,64,128]{2,1,0:T(8,128)S(1)} %copy-done.3, f32[19,64,128]{2,1,0:T(8,128)S(1)} %copy-done.4, f32[64,128]{1,0:T(8,128)S(1)} %copy-done.5, f32[64,128]{1,0:T(8,128)S(1)} %copy-done.6, ...), custom_call_target="tpu_custom_call" | custom-call | tf_op jit(solution)/shard_map/pallas_call | solution.py:340
  37.4 0.8 %copy.12 = f32[20,64,128]{2,1,0:T(8,128)} copy(f32[20,64,128]{2,1,0:T(8,128)S(1)} %shard_map.91) | data formatting | bytes 1310720
Async XLA Ops:
  0.8 1.3 %copy-start = (bf16[4,20,64,128]{3,2,1,0:T(8,128)(2,1)S(1)}, bf16[4,20,64,128]{3,2,1,0:T(8,128)(2,1)}, u32[]{:S(2)}) copy-start(bf16[4,20,64,128]{3,2,1,0:T(8,128)(2,1)} %inv_h.1) | copy-start | bytes 3932164
  2.1 1.1 %copy-start.1 = (f32[20,64,128]{2,1,0:T(8,128)S(1)}, f32[20,64,128]{2,1,0:T(8,128)}, u32[]{:S(2)}) copy-start(f32[20,64,128]{2,1,0:T(8,128)} %right_h.1) | copy-start | bytes 1966084
  3.2 1.1 %copy-start.2 = (f32[20,64,128]{2,1,0:T(8,128)S(1)}, f32[20,64,128]{2,1,0:T(8,128)}, u32[]{:S(2)}) copy-start(f32[20,64,128]{2,1,0:T(8,128)} %prev_h.1) | copy-start | bytes 1966084
  4.3 1.1 %copy-start.3 = (f32[20,64,128]{2,1,0:T(8,128)S(1)}, f32[20,64,128]{2,1,0:T(8,128)}, u32[]{:S(2)}) copy-start(f32[20,64,128]{2,1,0:T(8,128)} %diag_h.1) | copy-start | bytes 1966084
  5.4 1.1 %copy-start.4 = (f32[19,64,128]{2,1,0:T(8,128)S(1)}, f32[19,64,128]{2,1,0:T(8,128)}, u32[]{:S(2)}) copy-start(f32[19,64,128]{2,1,0:T(8,128)} %vert_h.1) | copy-start | bytes 1867780
  6.4 0.8 %copy-start.5 = (f32[64,128]{1,0:T(8,128)S(1)}, f32[64,128]{1,0:T(8,128)}, u32[]{:S(2)}) copy-start(f32[64,128]{1,0:T(8,128)} %ma_h.1) | copy-start | bytes 98308
  7.2 0.8 %copy-start.6 = (f32[64,128]{1,0:T(8,128)S(1)}, f32[64,128]{1,0:T(8,128)}, u32[]{:S(2)}) copy-start(f32[64,128]{1,0:T(8,128)} %mb_h.1) | copy-start | bytes 98308
  8.0 0.7 %copy-start.7 = (f32[20]{0:T(128)S(1)}, f32[20]{0:T(128)}, u32[]{:S(2)}) copy-start(f32[20]{0:T(128)} %prof_s.1) | copy-start | bytes 244

commit v2 on v1

--- a/solution.py
+++ b/solution.py
@@ -40,13 +40,13 @@
 
 def kernel(
     n_panel, n_gx,
-    right_h, prev_h, diag_h, vert_h, ma_h, mb_h, prof_s, inv_h, turn_s,
+    right_h, prev_h, diag_h, vert_h, ma_h, mb_h, prof_h, inv_h, turn_h,
     out_ref,
     rs, pp, ss, ww, rr, qq, dg, vt, ma, mb, inv,
     sf, sl, sb, rl, rh, bl, bh, wpk, nma_v, nmb_v,
     row_out, row_in,
     in_sem, rf_send, rl_send, rl_recv, rh_recv, bu_send, bd_send, bl_recv, bh_recv,
-    ar_send, ar_recv,
+    ar_send, ar_recv, prof_s, turn_s,
 ):
     levels, ta, tb = rs.shape
     n_dev = n_panel * n_gx
@@ -65,6 +65,8 @@
         pltpu.make_async_copy(vert_h, vt, in_sem.at[4]),
         pltpu.make_async_copy(right_h, rs, in_sem.at[5]),
         pltpu.make_async_copy(inv_h, inv, in_sem.at[6]),
+        pltpu.make_async_copy(prof_h, prof_s, in_sem.at[7]),
+        pltpu.make_async_copy(turn_h, turn_s, in_sem.at[8]),
     ]
     for load in loads:
         load.start()
@@ -80,9 +82,6 @@
 
     lax.fori_loop(1, n_dev, greet, 0)
 
-    t0, t1, t2, t3 = (turn_s[e, g, q] for e in range(4))
-    t0n = turn_s[0, g_next, q]
-    t2n = turn_s[2, g, q_next]
     rows_shape = sf.shape[1:]
     cols_shape = (ta, tb)
 
@@ -221,6 +220,9 @@
     send_cols(0)
     for load in loads[3:]:
         load.wait()
+    t0, t1, t2, t3 = (turn_s[e, q, g] for e in range(4))
+    t0n = turn_s[0, q, g_next]
+    t2n = turn_s[2, q_next, g]
     receive(0, pp)
 
     def first(c, carry):
@@ -335,12 +337,12 @@
         dma = pltpu.SemaphoreType.DMA
         field = vmem((levels, ta, tb), F32)
         padded = vmem((levels, ta + 2 * PAD, tb), F32)
-        any_spec = pl.BlockSpec(memory_space=pl.ANY)
-        smem_spec = pl.BlockSpec(memory_space=pltpu.SMEM)
+        any_spec = pl.BlockSpec(memory_space=pltpu.HBM)
+        turn = jnp.transpose(turn, (0, 2, 1))
         return pl.pallas_call(
             functools.partial(kernel, n_panel, n_gx),
             out_shape=jax.ShapeDtypeStruct((levels, ta, tb), F32),
-            in_specs=[any_spec] * 6 + [smem_spec, any_spec, smem_spec],
+            in_specs=[any_spec] * 9,
             out_specs=pl.BlockSpec(memory_space=pltpu.VMEM),
             scratch_shapes=[
                 field, padded, padded, padded, field, field, field,
@@ -360,12 +362,13 @@
                 vmem((ta, tb), F32),
                 vmem((1, tb), F32),
                 vmem((n_dev - 1, 1, tb), F32),
-                dma((7,)), dma((3,)), dma((3,)), dma((3,)), dma((3,)),
+                dma((9,)), dma((3,)), dma((3,)), dma((3,)), dma((3,)),
                 dma((3,)), dma((3,)), dma((3,)), dma((3,)),
                 dma, dma,
+                pltpu.SMEM(profile.shape, F32), pltpu.SMEM(turn.shape, jnp.int32),
             ],
             compiler_params=pltpu.CompilerParams(
-                collective_id=0, has_side_effects=True, vmem_limit_bytes=32 * 1024 * 1024
+                collective_id=0, has_side_effects=True, vmem_limit_bytes=60 * 1024 * 1024
             ),
         )(right_side, previous, diagonal, vertical, metric_a, metric_b, profile, inverse, turn)
 

time: 38.7 us -> 29.9 us (0.77)
  local copies, waits for them, and re-layouts: 9.44 us -> 1.99 us
  Pallas kernels: 28.8 us -> 27.8 us
    unnamed x18 -> x1, local copies, waits for them, and re-layouts: 9.44 us -> 1.99 us
    pallas_call x1, Pallas kernels: 28.8 us -> 27.8 us  [shards(): pl.pallas_call(functools.partial(kernel, n_panel, n_gx), out_shape=jax.Sh...]
where the time goes in v2:
time: 29.9 us; the launch traced here: 29.8 us
  Pallas kernels  27.8 us (93%)
  local copies, waits for them, and re-layouts  1.99 us (7%)
    pallas_call x1, Pallas kernels, shards(): pl.pallas_call(functools.partial(kernel, n_panel, n_gx), out_shape=jax.Sh...  27.8 us
    unnamed x1, local copies, waits for them, and re-layouts  1.99 us

profile of v2, /device:TPU:0, one launch (start us, length us, event | category | flops | bytes accessed | tf_op | source)
XLA Modules:
  0.0 29.8 jit_solution(1839784175811556341)
XLA Ops:
  0.0 27.8 %shard_map.91 = f32[20,64,128]{2,1,0:T(8,128)} custom-call(f32[20,64,128]{2,1,0:T(8,128)} %right_h.1, f32[20,64,128]{2,1,0:T(8,128)} %prev_h.1, f32[20,64,128]{2,1,0:T(8,128)} %diag_h.1, f32[19,64,128]{2,1,0:T(8,128)} %vert_h.1, f32[64,128]{1,0:T(8,128)} %ma_h.1, f32[64,128]{1,0:T(8,128)} %mb_h.1, f32[20]{0:T(128)} %prof_h.1, ...), custom_call_target="tpu_custom_call" | custom-call | tf_op jit(solution)/shard_map/pallas_call | solution.py:342
  27.8 2.0 %copy.11 = f32[20,64,128]{2,1,0:T(8,128)} copy(f32[20,64,128]{2,1,0:T(8,128)} %shard_map.91) | data formatting | bytes 1310720
